TPU v7x, 256 devices: a whole 4x4x8 slice. The times are simulated.
256 devices in a mesh: dp: 32 (over x, z), tensor: 8 (over y, core).
Axes of the slice: x: 4, y: 4, z: 8, core: 2. Of those that a mesh axis runs over, the one named last changes fastest.
Arguments:
- context: bfloat16 [2, 32768, 3072], P(None, 'dp', 'tensor'), may hold values from -6 to 6
- out_grad: bfloat16 [2, 32768, 3072], P(None, ('dp', 'tensor')), may hold values from -0.1875 to 0.1875
- error_in: bfloat16 [2, 98304, 3072], P(None, 'dp', 'tensor'), may hold values from -6 to 6
- right_init: float32 [2, 64, 3072], P(None, None, 'tensor'), may hold values from -6 to 6
Outputs:
- summed_update: bfloat16 [2, 3072, 3072], P(None, 'dp', 'tensor')
- error_out: bfloat16 [2, 98304, 3072], P(None, 'dp', 'tensor')
All inputs are finite; a program needn't handle non-finite values.
Results may differ from a plain program's by a relative error of at most 0.015.
Values may be sent and summed in bfloat16 or wider, within the bound.
No kernel may reach another device: no remote copies, remote signals or barrier semaphores. Data moves between devices by JAX's collectives and lax.ppermute only.
A program may use at most 128 MiB of HBM per device.

v0:
```python
import jax
import jax.numpy as jnp
from jax import lax
from jax.sharding import Mesh
from jax.sharding import PartitionSpec as P

TENSOR = ("tensor_0", "tensor_1")
DP_TENSOR = ("dp_0", "dp_1", "tensor_0", "tensor_1")
DP = ("dp_0", "dp_1")


def cut_along(x, dim, devices):
    dims = x.shape
    parts = x.reshape(*dims[:dim], devices, dims[dim] // devices, *dims[dim + 1 :])
    return jnp.moveaxis(parts, dim, 0)


def sent_and_summed(x, axis, dim):
    devices = lax.axis_size(axis)
    parts = lax.all_to_all(cut_along(x, dim, devices), axis, 0, 0, tiled=True)
    return jnp.sum(parts, axis=0)


def sum_in_two_steps(x, axes, dim):
    far, near = axes
    own = sent_and_summed(cut_along(x, dim, lax.axis_size(far)), near, dim + 1)
    return jnp.sum(lax.all_to_all(own, far, 0, 0, tiled=True), axis=0)


def filled_up(lines, devices):
    spare = -lines.shape[0] % devices
    if not spare:
        return lines
    return jnp.concatenate([lines, jnp.zeros((spare, *lines.shape[1:]), lines.dtype)])


def copy_for_each(x, axis):
    devices = lax.axis_size(axis)
    return lax.all_to_all(jnp.broadcast_to(x[None], (devices, *x.shape)), axis, 0, 0, tiled=True)


def joined_along(parts, dim):
    dims = list(parts.shape[1:])
    dims[dim] *= parts.shape[0]
    return jnp.moveaxis(parts, 0, dim).reshape(dims)


def gathered_by_axis(x, axes, dim):
    far, near = axes
    initial = copy_for_each(x, far)
    parts = jnp.swapaxes(copy_for_each(initial, near), 0, 1)
    return joined_along(parts.reshape(-1, *x.shape), dim)


def nested_sum(x, axes):
    lines = x.reshape(-1)
    own = sum_in_two_steps(
        filled_up(lines, lax.axis_size(axes[0]) * lax.axis_size(axes[1])), axes, 0
    )
    whole = gathered_by_axis(own, axes, 0)
    return whole[: len(lines)].reshape(x.shape)


def gathered_copies(x, axis, dim):
    return joined_along(copy_for_each(x, axis), dim)


def summed_on_arrival(x, axis, dim):
    parts = cut_along(x, dim, lax.axis_size(axis))
    arrived = lax.all_to_all(parts, axis, split_axis=0, concat_axis=0, tiled=True)
    return arrived.astype(jnp.float32).sum(axis=0)


def nested_sum_2(x, axes):
    lines = x.reshape(-1, x.shape[-1])
    padded = filled_up(lines, lax.axis_size(axes))
    whole = gathered_copies(summed_on_arrival(padded, axes, 0).astype(jnp.bfloat16), axes, 0)
    return lax.slice_in_dim(whole, 0, len(lines)).reshape(x.shape).astype(jnp.float32)


def solve_rows(gram_matrix, left_factor):
    ridge_term = 1e-06 * jnp.mean(jnp.diagonal(gram_matrix, axis1=1, axis2=2), axis=1)
    eye_matrix = jnp.eye(gram_matrix.shape[1], dtype=gram_matrix.dtype)
    gram_matrix = gram_matrix + ridge_term[:, None, None] * eye_matrix
    factor_low = jnp.linalg.cholesky(gram_matrix)

    def one_solve(low_part, rhs_part):
        return jax.scipy.linalg.solve_triangular(low_part, rhs_part, lower=True)

    return jax.vmap(one_solve)(factor_low, left_factor)


def gram_of(left_factor):
    return jnp.einsum("lrd,lsd->lrs", left_factor, left_factor, precision=lax.Precision.HIGHEST)


def compress(context, out_grad, error_in, right_init):
    out_width = out_grad.shape[2]
    moment = jnp.einsum(
        "ltd,lte->lde",
        lax.all_gather(out_grad, TENSOR, axis=1, tiled=True),
        context,
        preferred_element_type=jnp.float32,
    )
    moment = moment + error_in.astype(jnp.float32)
    left_factor = jnp.einsum("lre,lde->lrd", right_init, moment, precision=lax.Precision.HIGHEST)
    left_factor = nested_sum(left_factor, (("dp_0", "dp_1"), ("tensor_0", "tensor_1")))
    ortho_basis = solve_rows(gram_of(left_factor), left_factor)
    right_terms = jnp.einsum("lrd,lde->lre", ortho_basis, moment, precision=lax.Precision.HIGHEST)
    right_factor = nested_sum_2(right_terms.astype(jnp.bfloat16), DP)
    replicas = lax.axis_size(DP)
    row_share = out_width // replicas
    own_basis = lax.dynamic_slice_in_dim(ortho_basis, lax.axis_index(DP) * row_share, row_share, 2)
    summed = jnp.einsum("lrd,lre->lde", own_basis, right_factor, precision=lax.Precision.HIGHEST)
    mean_part = jnp.einsum(
        "lrd,lre->lde", ortho_basis, right_factor / replicas, precision=lax.Precision.HIGHEST
    )
    new_error = (moment - mean_part).astype(jnp.bfloat16)
    return (summed.astype(jnp.bfloat16), new_error)


def body(context, out_grad, error_in, right_init):
    return compress(context, out_grad, error_in, right_init)


def solution(mesh):
    finer = Mesh(mesh.devices.reshape(4, 8, 4, 2), ("dp_0", "dp_1", "tensor_0", "tensor_1"))
    return jax.shard_map(
        body,
        mesh=finer,
        in_specs=(
            P(None, DP, TENSOR),
            P(None, DP_TENSOR, None),
            P(None, DP, TENSOR),
            P(None, None, TENSOR),
        ),
        out_specs=(P(None, DP, TENSOR), P(None, DP, TENSOR)),
        check_vma=False,
    )
```

profile of v0, /device:TPU:2, one launch (start us, length us, event | category | flops | bytes accessed | tf_op | source)
XLA Modules:
  0.0 293.3 jit_solution(1838412830930112913)
XLA Ops:
  7.2 2.7 copy.16
  9.9 77.6 %all-gather.2.cloned.1.call-done = bf16[2,1024,3072]{1,2,0:T(8,128)(2,1)} async-done(((bf16[2,128,3072]{1,2,0:T(8,128)(2,1)}), bf16[2,1024,3072]{1,2,0:T(8,128)(2,1)}) %all-gather.2.cloned.1.call-update) | async-done | bytes 12582928 | tf_op jit(solution)/shard_map/all_gather | solution.py:101
  87.5 10.4 %convert_add_fusion = f32[2,3072,384]{2,1,0:T(8,128)S(1)} fusion(bf16[2,3072,384]{2,1,0:T(8,128)(2,1)} %param.6, bf16[2,1024,3072]{1,2,0:T(8,128)(2,1)} %all-gather.2.cloned.1.call-done, bf16[2,1024,384]{2,1,0:T(8,128)(2,1)S(1)} %copy-done), kind=kOutput, calls=%fused_computation.2 | convolution fusion | flops 4836556800 | bytes 28311552 | tf_op jit(solution)/shard_map/ltd,lte->lde/dot_general | solution.py:99
  97.9 3.6 %copy-done.1 = f32[2,3072,384]{2,1,0:T(8,128)} copy-done((f32[2,3072,384]{2,1,0:T(8,128)}, f32[2,3072,384]{2,1,0:T(8,128)S(1)}, u32[]{:S(2)}) %copy-start.1) | copy-done | bytes 9437208
  101.6 10.7 %convolution_bitcast_fusion = f32[2,64,3072]{2,1,0:T(8,128)} fusion(f32[2,3072,384]{2,1,0:T(8,128)S(1)} %convert_add_fusion, f32[2,64,384]{2,1,0:T(8,128)S(1)} %copy-done.3), kind=kOutput, calls=%fused_computation.3 | convolution fusion | flops 1811939328 | bytes 11206656 | tf_op jit(solution)/shard_map/lre,lde->lrd/dot_general | solution.py:106
  112.3 1.7 reshape_reshape_reshape.6
  114.9 25.4 %all_to_all.35 = f32[8,32,1536]{2,1,0:T(8,128)S(1)} all-to-all(f32[8,32,1536]{2,1,0:T(8,128)S(1)} %bitcast.34), channel_id=1, replica_groups=mesh['dp_0'=4,'dp_1'=8,'tensor_0'=4,'tensor_1'=2] {'tensor_0','tensor_1'}, dimensions={0} | all-to-all | bytes 3145728 | tf_op jit(solution)/shard_map/all_to_all | solution.py:20
  140.5 19.7 %all_to_all.36 = f32[32,1,1536]{2,1,0:T(1,128)S(1)} all-to-all(f32[32,1,1536]{2,1,0:T(1,128)S(1)} %all_to_all.23), channel_id=1, replica_groups=mesh['dp_0'=4,'dp_1'=8,'tensor_0'=4,'tensor_1'=2] {'dp_0','dp_1'}, dimensions={0} | all-to-all | bytes 393216 | tf_op jit(solution)/shard_map/all_to_all | solution.py:27
  160.5 14.6 %all_to_all.37 = f32[32,1,1536]{2,1,0:T(1,128)S(1)} all-to-all(f32[32,1,1536]{2,1,0:T(1,128)S(1)} %broadcast_in_dim.14), channel_id=1, replica_groups=mesh['dp_0'=4,'dp_1'=8,'tensor_0'=4,'tensor_1'=2] {'dp_0','dp_1'}, dimensions={0} | all-to-all | bytes 393216 | tf_op jit(solution)/shard_map/all_to_all | solution.py:39
  176.4 3.6 %all-to-all-start.3 = ((f32[8,32,1536]{2,1,0:T(8,128)}), f32[8,32,1536]{2,1,0:T(8,128)S(1)}, u32[]{:S(2)}, u32[]{:S(2)}) async-start(f32[8,32,1536]{2,1,0:T(8,128)} %broadcast_in_dim.18), calls=%async_computation.3 | async-start | bytes 3145728 | tf_op jit(solution)/shard_map/all_to_all | solution.py:39
  180.1 21.4 %all-to-all-done.3 = f32[8,32,1536]{2,1,0:T(8,128)S(1)} async-done(((f32[8,32,1536]{2,1,0:T(8,128)}), f32[8,32,1536]{2,1,0:T(8,128)S(1)}, u32[]{:S(2)}, u32[]{:S(2)}) %all-to-all-start.3) | async-done | bytes 1572896 | tf_op jit(solution)/shard_map/all_to_all | solution.py:39
  201.5 2.1 copy.18
  203.5 1.8 reshape_reshape_reshape.7
  205.3 1.6 fusion.12
  206.9 2.0 copy.19
  209.0 1.6 gather_fusion
  210.7 11.7 %custom-call.8 = f32[2,64,64]{2,1,0:T(8,128)S(1)} custom-call(f32[2,64,64]{2,1,0:T(8,128)S(1)} %fusion.6), custom_call_target="Cholesky" | custom-call | tf_op jit(solution)/shard_map/jit(cholesky)/cholesky | solution.py:85
  222.7 9.8 %custom-call.9 = f32[2,1,64,64]{2,3,1,0:T(8,128)S(1)} custom-call(f32[2,1,64,64]{3,2,1,0:T(8,128)S(1)} %select_bitcast_fusion), custom_call_target="InvertDiagBlocksLowerTriangular" | custom-call | tf_op jit(solution)/shard_map/vmap(jit(_solve_triangular))/triangular_solve | solution.py:88
  235.2 8.2 %convolution_convert_fusion.1 = bf16[2,64,384]{2,1,0:T(8,128)(2,1)S(1)} fusion(f32[2,64,3072]{2,1,0:T(8,128)S(1)} %fusion.3, f32[2,3072,384]{2,1,0:T(8,128)} %copy-done.1), kind=kOutput, calls=%fused_computation.6 | convolution fusion | flops 1811988480 | bytes 11108352 | tf_op jit(solution)/shard_map/lrd,lde->lre/dot_general | solution.py:109
  243.4 14.0 %all_to_all.38 = bf16[32,4,384]{2,1,0:T(4,128)(2,1)S(1)} all-to-all(bf16[32,4,384]{2,1,0:T(4,128)(2,1)S(1)} %reshape_reshape.6), channel_id=1, replica_groups=mesh['dp_0'=4,'dp_1'=8,'tensor_0'=4,'tensor_1'=2] {'dp_0','dp_1'}, dimensions={0} | all-to-all | bytes 196608 | tf_op jit(solution)/shard_map/all_to_all | solution.py:70
  258.2 5.0 %all-to-all-start.5 = ((bf16[32,4,384]{2,1,0:T(4,128)(2,1)}), bf16[32,4,384]{2,1,0:T(4,128)(2,1)S(1)}, u32[]{:S(2)}, u32[]{:S(2)}) async-start(bf16[32,4,384]{2,1,0:T(4,128)(2,1)} %broadcast_in_dim.19), calls=%async_computation.5 | async-start | bytes 196608 | tf_op jit(solution)/shard_map/all_to_all | solution.py:39
  263.2 9.1 %all-to-all-done.5 = bf16[32,4,384]{2,1,0:T(4,128)(2,1)S(1)} async-done(((bf16[32,4,384]{2,1,0:T(4,128)(2,1)}), bf16[32,4,384]{2,1,0:T(4,128)(2,1)S(1)}, u32[]{:S(2)}, u32[]{:S(2)}) %all-to-all-start.5) | async-done | bytes 98336 | tf_op jit(solution)/shard_map/all_to_all | solution.py:39
  272.3 12.1 %subtract_convert_fusion = bf16[2,3072,384]{2,1,0:T(8,128)(2,1)} fusion(f32[2,3072,384]{2,1,0:T(8,128)} %copy-done.1, f32[2,64,3072]{2,1,0:T(8,128)} %copy-done.2, bf16[2,64,384]{2,1,0:T(8,128)(2,1)S(1)} %reshape_reshape.7), kind=kOutput, calls=%fused_computation.1 | convolution fusion | flops 1816756224 | bytes 15826944 | tf_op jit(solution)/shard_map/lrd,lre->lde/dot_general | solution.py:115
  284.5 2.0 convolution_convert_fusion
  (32 shorter events, 6.7 us)
Async XLA Ops:
  7.2 80.4 %copy-start = (bf16[2,1024,384]{2,1,0:T(8,128)(2,1)S(1)}, bf16[2,1024,384]{2,1,0:T(8,128)(2,1)}, u32[]{:S(2)}) copy-start(bf16[2,1024,384]{2,1,0:T(8,128)(2,1)} %param.4) | copy-start | bytes 4718596
  7.2 80.3 %all-gather.2.cloned.1.call-start = ((), (), s32[]{:S(2)}) async-start(), calls=%async_computation.6 | async-start | bytes 14155776 | tf_op jit(solution)/shard_map/all_gather | solution.py:101
  9.9 91.6 %copy-start.3 = (f32[2,64,384]{2,1,0:T(8,128)S(1)}, f32[2,64,384]{2,1,0:T(8,128)}, u32[]{:S(2)}) copy-start(f32[2,64,384]{2,1,0:T(8,128)} %param.7) | copy-start | bytes 589828
  97.9 3.6 %copy-start.1 = (f32[2,3072,384]{2,1,0:T(8,128)}, f32[2,3072,384]{2,1,0:T(8,128)S(1)}, u32[]{:S(2)}) copy-start(f32[2,3072,384]{2,1,0:T(8,128)S(1)} %convert_add_fusion) | copy-start | bytes 28311556
  176.4 25.1 %all-to-all-start.3 = ((f32[8,32,1536]{2,1,0:T(8,128)}), f32[8,32,1536]{2,1,0:T(8,128)S(1)}, u32[]{:S(2)}, u32[]{:S(2)}) async-start(f32[8,32,1536]{2,1,0:T(8,128)} %broadcast_in_dim.18), calls=%async_computation.3 | async-start | bytes 3145728 | tf_op jit(solution)/shard_map/all_to_all | solution.py:39
  234.1 1.2 copy-start.2
  258.2 14.1 %all-to-all-start.5 = ((bf16[32,4,384]{2,1,0:T(4,128)(2,1)}), bf16[32,4,384]{2,1,0:T(4,128)(2,1)S(1)}, u32[]{:S(2)}, u32[]{:S(2)}) async-start(bf16[32,4,384]{2,1,0:T(4,128)(2,1)} %broadcast_in_dim.19), calls=%async_computation.5 | async-start | bytes 196608 | tf_op jit(solution)/shard_map/all_to_all | solution.py:39
Sparse Core Ops, SparseCore 0:
  10.4 77.0 all-gather.1
where the time goes:
time: 294 us; the launch traced here: 293 us
  waiting for transfers between devices  108 us (37%)
  blocking collectives  73.7 us (25%)
  matrix products  46.4 us (16%)
  other arithmetic  22.2 us (8%)
  local copies, waits for them, and re-layouts  20 us (7%)
  between operations  14.2 us (5%)
  starting transfers between devices  8.59 us (3%)
    all_gather x1, waiting for transfers between devices, compress(): lax.all_gather(out_grad, TENSOR, axis=1, tiled=True)  77.6 us
    all_to_all x2, waiting for transfers between devices, copy_for_each(): lax.all_to_all(jnp.broadcast_to(x[None], (devices, *x.shape)), axis, 0, 0...  30.5 us
    all_to_all x1, blocking collectives, sent_and_summed(): parts = lax.all_to_all(cut_along(x, dim, devices), axis, 0, 0, tiled=True)  25.4 us
    all_to_all x1, blocking collectives, sum_in_two_steps(): return jnp.sum(lax.all_to_all(own, far, 0, 0, tiled=True), axis=0)  19.7 us
    all_to_all x1, blocking collectives, copy_for_each(): lax.all_to_all(jnp.broadcast_to(x[None], (devices, *x.shape)), axis, 0, 0...  14.6 us
    all_to_all x1, blocking collectives, summed_on_arrival(): lax.all_to_all(parts, axis, split_axis=0, concat_axis=0, tiled=True)  14 us
    dot_general x1, matrix products, compress(): jnp.einsum('lrd,lre->lde', ortho_basis, right_factor / replicas, precisio...  12.1 us
    another operation x4, other arithmetic, solve_rows(): factor_low = jnp.linalg.cholesky(gram_matrix)  11.9 us
  transfers between devices with their start and end apart: 3, of which 3 were waited for; matrix products, arithmetic and copies ran while one was open for 0% of the time, Pallas kernels for 0%

commit v1 on v0

--- a/solution.py
+++ b/solution.py
@@ -7,6 +7,11 @@
 TENSOR = ("tensor_0", "tensor_1")
 DP_TENSOR = ("dp_0", "dp_1", "tensor_0", "tensor_1")
 DP = ("dp_0", "dp_1")
+
+
+def swapped_in(array, axis, d):
+    sent = jnp.stack([array] * lax.axis_size(axis))
+    return jnp.concatenate(lax.all_to_all(sent, axis, 0, 0), axis=d)
 
 
 def cut_along(x, dim, devices):
@@ -97,10 +102,7 @@
 def compress(context, out_grad, error_in, right_init):
     out_width = out_grad.shape[2]
     moment = jnp.einsum(
-        "ltd,lte->lde",
-        lax.all_gather(out_grad, TENSOR, axis=1, tiled=True),
-        context,
-        preferred_element_type=jnp.float32,
+        "ltd,lte->lde", swapped_in(out_grad, TENSOR, 1), context, preferred_element_type=jnp.float32
     )
     moment = moment + error_in.astype(jnp.float32)
     left_factor = jnp.einsum("lre,lde->lrd", right_init, moment, precision=lax.Precision.HIGHEST)

time: 294 us -> 349 us (1.19)
  blocking collectives: 73.7 us -> 221 us
  waiting for transfers between devices: 108 us -> 30.3 us
  between operations: 14.2 us -> 0.82 us
    all_to_all x0 -> x1, blocking collectives: none -> 146 us  [swapped_in(): return jnp.concatenate(lax.all_to_all(sent, axis, 0, 0), axis=d)]
    all_gather x1 -> x0, waiting for transfers between devices: 77.6 us -> none  [compress(): lax.all_gather(out_grad, TENSOR, axis=1, tiled=True)]
    another operation x0 -> x1, local copies, waits for them, and re-layouts: none -> 7 us  [swapped_in(): sent = jnp.stack([array] * lax.axis_size(axis))]
  transfers between devices with their start and end apart: 3 -> 2, of which waited for: 3 -> 2; matrix products, arithmetic and copies ran while one was open for 0% -> 0% of each run, Pallas kernels for 0% -> 0%
where the time goes in v1:
time: 349 us
  blocking collectives  221 us (63%)
  matrix products  44.4 us (13%)
  waiting for transfers between devices  30.3 us (9%)
  other arithmetic  22.2 us (6%)
  local copies, waits for them, and re-layouts  21.2 us (6%)
  starting transfers between devices  8.78 us (3%)
    all_to_all x1, blocking collectives, swapped_in(): return jnp.concatenate(lax.all_to_all(sent, axis, 0, 0), axis=d)  146 us
    all_to_all x2, waiting for transfers between devices, copy_for_each(): lax.all_to_all(jnp.broadcast_to(x[None], (devices, *x.shape)), axis, 0, 0...  30.3 us
    all_to_all x1, blocking collectives, sent_and_summed(): parts = lax.all_to_all(cut_along(x, dim, devices), axis, 0, 0, tiled=True)  25 us
    all_to_all x1, blocking collectives, sum_in_two_steps(): return jnp.sum(lax.all_to_all(own, far, 0, 0, tiled=True), axis=0)  21.2 us
    all_to_all x1, blocking collectives, copy_for_each(): lax.all_to_all(jnp.broadcast_to(x[None], (devices, *x.shape)), axis, 0, 0...  14.6 us
    all_to_all x1, blocking collectives, summed_on_arrival(): lax.all_to_all(parts, axis, split_axis=0, concat_axis=0, tiled=True)  14 us
    another operation x4, other arithmetic, solve_rows(): factor_low = jnp.linalg.cholesky(gram_matrix)  11.9 us
    dot_general x1, matrix products, compress(): jnp.einsum('lrd,lre->lde', ortho_basis, right_factor / replicas, precisio...  11.6 us
  transfers between devices with their start and end apart: 2, of which 2 were waited for; matrix products, arithmetic and copies ran while one was open for 0% of the time, Pallas kernels for 0%

profile of v1, /device:TPU:2, one launch (start us, length us, event | category | flops | bytes accessed | tf_op | source)
XLA Modules:
  0.0 348.9 jit_solution(12536229819782741604)
XLA Ops:
  0.6 2.0 copy.17
  2.7 7.0 %stack.2 = bf16[8,2,128,3072]{2,3,1,0:T(8,128)(2,1)} broadcast(bf16[2,128,3072]{1,2,0:T(8,128)(2,1)S(1)} %copy.17), dimensions={1,2,3} | broadcast | bytes 14155776 | tf_op jit(solution)/shard_map/stack | solution.py:13
  9.7 146.3 %all_to_all.40 = bf16[8,2,128,3072]{2,3,1,0:T(8,128)(2,1)} all-to-all(bf16[8,2,128,3072]{2,3,1,0:T(8,128)(2,1)} %stack.2), channel_id=1, replica_groups=mesh['dp_0'=4,'dp_1'=8,'tensor_0'=4,'tensor_1'=2] {'tensor_0','tensor_1'}, dimensions={0} | all-to-all | bytes 25165824 | tf_op jit(solution)/shard_map/all_to_all | solution.py:14
  156.0 11.0 %convert_add_fusion = f32[2,3072,384]{2,1,0:T(8,128)S(1)} fusion(bf16[2,3072,384]{2,1,0:T(8,128)(2,1)} %param.6, bf16[2,1024,384]{2,1,0:T(8,128)(2,1)S(1)} %copy-done, bf16[8,2,128,3072]{2,3,1,0:T(8,128)(2,1)} %all_to_all.40), kind=kOutput, calls=%fused_computation.5 | convolution fusion | flops 4836556800 | bytes 28311552 | tf_op jit(solution)/shard_map/ltd,lte->lde/dot_general | solution.py:104
  167.0 3.6 %copy-done.2 = f32[2,3072,384]{2,1,0:T(8,128)} copy-done((f32[2,3072,384]{2,1,0:T(8,128)}, f32[2,3072,384]{2,1,0:T(8,128)S(1)}, u32[]{:S(2)}) %copy-start.2) | copy-done | bytes 9437208
  170.6 9.5 %convolution_bitcast_fusion = f32[2,64,3072]{2,1,0:T(8,128)S(1)} fusion(f32[2,3072,384]{2,1,0:T(8,128)S(1)} %convert_add_fusion, f32[2,64,384]{2,1,0:T(8,128)S(1)} %copy-done.3), kind=kOutput, calls=%fused_computation.6 | convolution fusion | flops 1811939328 | bytes 11206656 | tf_op jit(solution)/shard_map/lre,lde->lrd/dot_general | solution.py:108
  181.3 25.0 %all_to_all.41 = f32[8,32,1536]{2,1,0:T(8,128)S(1)} all-to-all(f32[8,32,1536]{2,1,0:T(8,128)S(1)} %bitcast.43), channel_id=1, replica_groups=mesh['dp_0'=4,'dp_1'=8,'tensor_0'=4,'tensor_1'=2] {'tensor_0','tensor_1'}, dimensions={0} | all-to-all | bytes 3145728 | tf_op jit(solution)/shard_map/all_to_all | solution.py:25
  206.6 21.2 %all_to_all.42 = f32[32,1,1536]{2,1,0:T(1,128)S(1)} all-to-all(f32[32,1,1536]{2,1,0:T(1,128)S(1)} %all_to_all.27), channel_id=1, replica_groups=mesh['dp_0'=4,'dp_1'=8,'tensor_0'=4,'tensor_1'=2] {'dp_0','dp_1'}, dimensions={0} | all-to-all | bytes 393216 | tf_op jit(solution)/shard_map/all_to_all | solution.py:32
  228.0 14.6 %all_to_all.43 = f32[32,1,1536]{2,1,0:T(1,128)S(1)} all-to-all(f32[32,1,1536]{2,1,0:T(1,128)S(1)} %broadcast_in_dim.14), channel_id=1, replica_groups=mesh['dp_0'=4,'dp_1'=8,'tensor_0'=4,'tensor_1'=2] {'dp_0','dp_1'}, dimensions={0} | all-to-all | bytes 393216 | tf_op jit(solution)/shard_map/all_to_all | solution.py:44
  242.6 1.3 broadcast_in_dim.18
  243.9 3.8 %all-to-all-start.4 = ((f32[8,32,1536]{2,1,0:T(8,128)}), f32[8,32,1536]{2,1,0:T(8,128)S(1)}, u32[]{:S(2)}, u32[]{:S(2)}) async-start(f32[8,32,1536]{2,1,0:T(8,128)} %broadcast_in_dim.18), calls=%async_computation.4 | async-start | bytes 3145728 | tf_op jit(solution)/shard_map/all_to_all | solution.py:44
  247.8 21.2 %all-to-all-done.4 = f32[8,32,1536]{2,1,0:T(8,128)S(1)} async-done(((f32[8,32,1536]{2,1,0:T(8,128)}), f32[8,32,1536]{2,1,0:T(8,128)S(1)}, u32[]{:S(2)}, u32[]{:S(2)}) %all-to-all-start.4) | async-done | bytes 1572896 | tf_op jit(solution)/shard_map/all_to_all | solution.py:44
  270.4 1.6 fusion.17
  272.0 2.0 copy.21
  274.1 1.6 gather_fusion
  275.8 11.7 %custom-call.8 = f32[2,64,64]{2,1,0:T(8,128)S(1)} custom-call(f32[2,64,64]{2,1,0:T(8,128)S(1)} %fusion.11), custom_call_target="Cholesky" | custom-call | tf_op jit(solution)/shard_map/jit(cholesky)/cholesky | solution.py:90
  287.8 9.8 %custom-call.9 = f32[2,1,64,64]{2,3,1,0:T(8,128)S(1)} custom-call(f32[2,1,64,64]{3,2,1,0:T(8,128)S(1)} %select_bitcast_fusion), custom_call_target="InvertDiagBlocksLowerTriangular" | custom-call | tf_op jit(solution)/shard_map/vmap(jit(_solve_triangular))/triangular_solve | solution.py:93
  297.6 1.5 fusion.8
  299.1 8.1 %convolution_convert_fusion.1 = bf16[2,64,384]{2,1,0:T(8,128)(2,1)S(1)} fusion(f32[2,64,3072]{2,1,0:T(8,128)S(1)} %fusion.8, f32[2,3072,384]{2,1,0:T(8,128)} %copy-done.2), kind=kOutput, calls=%fused_computation.9 | convolution fusion | flops 1811988480 | bytes 11108352 | tf_op jit(solution)/shard_map/lrd,lde->lre/dot_general | solution.py:111
  307.3 14.0 %all_to_all.44 = bf16[32,4,384]{2,1,0:T(4,128)(2,1)S(1)} all-to-all(bf16[32,4,384]{2,1,0:T(4,128)(2,1)S(1)} %reshape_reshape.6), channel_id=1, replica_groups=mesh['dp_0'=4,'dp_1'=8,'tensor_0'=4,'tensor_1'=2] {'dp_0','dp_1'}, dimensions={0} | all-to-all | bytes 196608 | tf_op jit(solution)/shard_map/all_to_all | solution.py:75
  322.1 5.0 %all-to-all-start.6 = ((bf16[32,4,384]{2,1,0:T(4,128)(2,1)}), bf16[32,4,384]{2,1,0:T(4,128)(2,1)S(1)}, u32[]{:S(2)}, u32[]{:S(2)}) async-start(bf16[32,4,384]{2,1,0:T(4,128)(2,1)} %broadcast_in_dim.19), calls=%async_computation.6 | async-start | bytes 196608 | tf_op jit(solution)/shard_map/all_to_all | solution.py:44
  327.1 9.1 %all-to-all-done.6 = bf16[32,4,384]{2,1,0:T(4,128)(2,1)S(1)} async-done(((bf16[32,4,384]{2,1,0:T(4,128)(2,1)}), bf16[32,4,384]{2,1,0:T(4,128)(2,1)S(1)}, u32[]{:S(2)}, u32[]{:S(2)}) %all-to-all-start.6) | async-done | bytes 98336 | tf_op jit(solution)/shard_map/all_to_all | solution.py:44
  336.2 11.6 %subtract_convert_fusion = bf16[2,3072,384]{2,1,0:T(8,128)(2,1)} fusion(f32[2,3072,384]{2,1,0:T(8,128)} %copy-done.2, f32[2,64,3072]{2,1,0:T(8,128)S(1)} %fusion.8, bf16[2,64,384]{2,1,0:T(8,128)(2,1)S(1)} %reshape_reshape.7), kind=kOutput, calls=%fused_computation.4 | convolution fusion | flops 1816756224 | bytes 15826944 | tf_op jit(solution)/shard_map/lrd,lre->lde/dot_general | solution.py:117
  347.8 1.1 convolution_convert_fusion
  (31 shorter events, 4.3 us)
Async XLA Ops:
  0.6 155.3 %copy-start = (bf16[2,1024,384]{2,1,0:T(8,128)(2,1)S(1)}, bf16[2,1024,384]{2,1,0:T(8,128)(2,1)}, u32[]{:S(2)}) copy-start(bf16[2,1024,384]{2,1,0:T(8,128)(2,1)} %param.4) | copy-start | bytes 4718596
  156.0 14.6 %copy-start.3 = (f32[2,64,384]{2,1,0:T(8,128)S(1)}, f32[2,64,384]{2,1,0:T(8,128)}, u32[]{:S(2)}) copy-start(f32[2,64,384]{2,1,0:T(8,128)} %param.7) | copy-start | bytes 589828
  167.0 3.6 %copy-start.2 = (f32[2,3072,384]{2,1,0:T(8,128)}, f32[2,3072,384]{2,1,0:T(8,128)S(1)}, u32[]{:S(2)}) copy-start(f32[2,3072,384]{2,1,0:T(8,128)S(1)} %convert_add_fusion) | copy-start | bytes 28311556
  243.9 25.1 %all-to-all-start.4 = ((f32[8,32,1536]{2,1,0:T(8,128)}), f32[8,32,1536]{2,1,0:T(8,128)S(1)}, u32[]{:S(2)}, u32[]{:S(2)}) async-start(f32[8,32,1536]{2,1,0:T(8,128)} %broadcast_in_dim.18), calls=%async_computation.4 | async-start | bytes 3145728 | tf_op jit(solution)/shard_map/all_to_all | solution.py:44
  322.1 14.1 %all-to-all-start.6 = ((bf16[32,4,384]{2,1,0:T(4,128)(2,1)}), bf16[32,4,384]{2,1,0:T(4,128)(2,1)S(1)}, u32[]{:S(2)}, u32[]{:S(2)}) async-start(bf16[32,4,384]{2,1,0:T(4,128)(2,1)} %broadcast_in_dim.19), calls=%async_computation.6 | async-start | bytes 196608 | tf_op jit(solution)/shard_map/all_to_all | solution.py:44
  336.2 12.7 %copy-start.1 = (bf16[2,1024,384]{2,1,0:T(8,128)(2,1)S(1)}, bf16[2,1024,384]{2,1,0:T(8,128)(2,1)}, u32[]{:S(2)}) copy-start(bf16[2,1024,384]{2,1,0:T(8,128)(2,1)} %param.4) | copy-start | bytes 4718596
